TPU v7x, 32 devices: a whole 2x2x4 slice. The times are simulated.
32 devices in a mesh: wide: 4 (over z), narrow: 8 (over y, x, core).
Axes of the slice: x: 2, y: 2, z: 4, core: 2. Of those that a mesh axis runs over, the one named last changes fastest.
Arguments:
- layer_entry_input: bfloat16 [4096, 2048], P('wide'), may hold values from -6 to 6
- ln1_gain: float32 [2048], replicated, may hold values from 0.5 to 1.5
- ln1_bias: float32 [2048], replicated, may hold values from -1 to 1
- w_qkv: bfloat16 [2048, 3, 2048], P(None, None, 'narrow'), may hold values from -0.125 to 0.125
- b_qv: float32 [2, 2048], P(None, 'narrow'), may hold values from -1.5 to 1.5
- w_out: bfloat16 [2048, 2048], P('narrow'), may hold values from -2 to 2
- b_out: float32 [2048], replicated, may hold values from -1.5 to 1.5
- ln2_gain: float32 [2048], replicated, may hold values from 0.5 to 1.5
- ln2_bias: float32 [2048], replicated, may hold values from -1 to 1
- w_up: bfloat16 [2048, 8192], P(None, 'narrow'), may hold values from -0.125 to 0.125
- b_up: float32 [8192], P('narrow'), may hold values from -2.5 to 2.5
- w_down: bfloat16 [8192, 2048], P('narrow'), may hold values from -0.0625 to 0.0625
- b_down: float32 [2048], replicated, may hold values from -1.5 to 1.5
- document_index: int32 [4096], replicated, may hold values from 0 to 8, as said below
- positions: int32 [4096], replicated, may hold values from 0 to 767, as said below
- valid: int32 [4096], replicated, may hold values from 0 to 1, as said below
- cotangent: bfloat16 [4096, 2048], P('wide'), may hold values from -6 to 6
Outputs:
- output: bfloat16 [4096, 2048], P('wide')
- grad_input: bfloat16 [4096, 2048], P('wide')
- grad_ln1_gain: float32 [2048], replicated
- grad_ln1_bias: float32 [2048], replicated
- grad_w_qkv: float32 [2048, 3, 2048], P(None, None, 'narrow')
- grad_b_qv: float32 [2, 2048], P(None, 'narrow')
- grad_w_out: float32 [2048, 2048], P('narrow')
- grad_b_out: float32 [2048], replicated
- grad_ln2_gain: float32 [2048], replicated
- grad_ln2_bias: float32 [2048], replicated
- grad_w_up: float32 [2048, 8192], P(None, 'narrow')
- grad_b_up: float32 [8192], P('narrow')
- grad_w_down: float32 [8192, 2048], P('narrow')
- grad_b_down: float32 [2048], replicated
Inputs may be any that keep to these rules, and one draw needn't show every extreme that they name: `document_index`: documents are contiguous and numbered in order from 0; each block of 1024 tokens of one index of wide holds exactly two document starts, and every document has at most 768 tokens. `positions`: counts from 0 at the first token of each document, padding included. `valid`: 0 exactly on the last 1 to 64 tokens of each document.
All inputs are finite; a program needn't handle non-finite values.
Results may differ from a plain program's by a relative error of at most 0.019.
Values may be sent and summed in bfloat16 or wider, within the bound.
No kernel may reach another device: no remote copies, remote signals or barrier semaphores. Data moves between devices by JAX's collectives and lax.ppermute only.
A program may use at most 192 MiB of HBM per device.

v0:
```python
import jax
import jax.numpy as jnp
from jax import lax
from jax.sharding import PartitionSpec as P

HEAD_DIM = 128
ROW_TOKENS = 2048


def from_behind(value, axis, steps):
    count = lax.axis_size(axis)
    initial, last = (max(0, -steps), min(count, count - steps))
    return lax.ppermute(value, axis, [(source, source + steps) for source in range(initial, last)])


def norm_stats(values):
    center = values - jnp.mean(values, axis=-1, keepdims=True)
    spread = jnp.mean(center * center, axis=-1, keepdims=True)
    inverse = lax.rsqrt(spread + 1e-05)
    return (center * inverse, inverse)


def norm_local(grad_out, normed_raw, inverse, gain):
    scaled = grad_out * gain
    grad_in = inverse * (
        scaled
        - jnp.mean(scaled, axis=-1, keepdims=True)
        - normed_raw * jnp.mean(scaled * normed_raw, axis=-1, keepdims=True)
    )
    return (grad_in, jnp.sum(grad_out * normed_raw, axis=0), jnp.sum(grad_out, axis=0))


def norm_back(partial_value, normed_raw, inverse, gain):
    summed = lax.psum(partial_value, "narrow")
    return norm_local(summed, normed_raw, inverse, gain)


def on_device(
    layer_entry_input,
    ln1_gain,
    ln1_bias,
    w_qkv,
    b_qv,
    w_out,
    b_out,
    ln2_gain,
    ln2_bias,
    w_up,
    b_up,
    w_down,
    b_down,
    document_index,
    positions,
    valid,
    cotangent,
):
    token_rows = layer_entry_input.shape[0]
    local_width = w_qkv.shape[2]
    head_count = local_width // HEAD_DIM
    document_spans = ROW_TOKENS // token_rows
    key_rows = document_spans * token_rows
    scale = HEAD_DIM ** (-0.5)
    start = lax.axis_index("wide") * token_rows
    query_index = start + jnp.arange(token_rows, dtype=jnp.int32)
    key_index = start - (document_spans - 1) * token_rows + jnp.arange(key_rows, dtype=jnp.int32)
    safe_index = jnp.clip(key_index, 0, document_index.shape[0] - 1)
    seg_query = lax.dynamic_slice_in_dim(document_index, start, token_rows, 0)
    pos_query = lax.dynamic_slice_in_dim(positions, start, token_rows, 0)
    seg_key = jnp.take(document_index, safe_index)
    pos_key = jnp.take(positions, safe_index)
    valid_key = jnp.take(valid, safe_index)
    allowed = (
        (key_index[None, :] >= 0)
        & (seg_key[None, :] == seg_query[:, None])
        & (pos_key[None, :] <= pos_query[:, None])
        & ((valid_key[None, :] == 1) | (key_index[None, :] == query_index[:, None]))
    )
    inputs = layer_entry_input.astype(jnp.float32)
    raw_one, inv_one = norm_stats(inputs)
    normed_one = (raw_one * ln1_gain + ln1_bias).astype(jnp.bfloat16)
    mixed = jnp.einsum("td,dch->tch", normed_one, w_qkv, preferred_element_type=jnp.float32)
    query = (mixed[:, 0] + b_qv[0]).astype(jnp.bfloat16)
    key_val = jnp.stack([mixed[:, 1], mixed[:, 2] + b_qv[1]]).astype(jnp.bfloat16)
    pieces = [key_val]
    current = key_val
    current = from_behind(current, "wide", 1)
    pieces.insert(0, current)
    joined = jnp.concatenate(pieces, axis=1)
    keys_heads = joined[0].reshape(key_rows, head_count, HEAD_DIM)
    vals_heads = joined[1].reshape(key_rows, head_count, HEAD_DIM)
    query_heads = query.reshape(token_rows, head_count, HEAD_DIM)

    def scores_of():
        raw = (
            jnp.einsum("qhd,khd->hqk", query_heads, keys_heads, preferred_element_type=jnp.float32)
            * scale
        )
        return jnp.where(allowed[None], raw, -1e30)

    scores = scores_of()
    row_max = jnp.max(scores, axis=-1, keepdims=True)
    log_total = row_max + jnp.log(jnp.sum(jnp.exp(scores - row_max), axis=-1, keepdims=True))
    probs = jnp.exp(scores - log_total)
    attended = jnp.einsum(
        "hqk,khd->qhd", probs.astype(jnp.bfloat16), vals_heads, preferred_element_type=jnp.float32
    )
    attended = attended.reshape(token_rows, local_width).astype(jnp.bfloat16)
    attn_total = lax.psum(
        jnp.dot(attended, w_out, preferred_element_type=jnp.float32).astype(jnp.bfloat16), "narrow"
    ).astype(jnp.float32)
    after_attn = inputs + b_out + attn_total
    raw_two, inv_two = norm_stats(after_attn)
    normed_two = (raw_two * ln2_gain + ln2_bias).astype(jnp.bfloat16)
    upper = jnp.dot(normed_two, w_up, preferred_element_type=jnp.float32) + b_up
    active, gelu_pull = jax.vjp(jax.nn.gelu, upper)
    active = active.astype(jnp.bfloat16)
    mlp_total = lax.psum(
        jnp.dot(active, w_down, preferred_element_type=jnp.float32).astype(jnp.bfloat16), "narrow"
    ).astype(jnp.float32)
    output = (after_attn + b_down + mlp_total).astype(jnp.bfloat16)
    grad_out = cotangent.astype(jnp.float32)
    grad_b_down = jnp.sum(grad_out, axis=0)
    grad_w_down = jnp.einsum("tf,td->fd", active, cotangent, preferred_element_type=jnp.float32)
    grad_active = jnp.einsum("td,fd->tf", cotangent, w_down, preferred_element_type=jnp.float32)
    grad_upper = gelu_pull(grad_active)[0].astype(jnp.bfloat16)
    grad_w_up = jnp.einsum("td,tf->df", normed_two, grad_upper, preferred_element_type=jnp.float32)
    grad_b_up = jnp.sum(grad_upper.astype(jnp.float32), axis=0)
    grad_norm_two = jnp.einsum("tf,df->td", grad_upper, w_up, preferred_element_type=jnp.float32)
    grad_resid_two, grad_ln2_gain, grad_ln2_bias = norm_back(
        grad_norm_two, raw_two, inv_two, ln2_gain
    )
    grad_mid = grad_out + grad_resid_two
    grad_b_out = jnp.sum(grad_mid, axis=0)
    grad_mid_low = grad_mid.astype(jnp.bfloat16)
    grad_w_out = jnp.einsum("th,td->hd", attended, grad_mid_low, preferred_element_type=jnp.float32)
    grad_attended = jnp.einsum(
        "td,hd->th", grad_mid_low, w_out, preferred_element_type=jnp.float32
    ).astype(jnp.bfloat16)
    grad_att_heads = grad_attended.reshape(token_rows, head_count, HEAD_DIM)
    probs_again = jnp.exp(scores_of() - log_total)
    grad_vals = jnp.einsum(
        "hqk,qhd->khd",
        probs_again.astype(jnp.bfloat16),
        grad_att_heads,
        preferred_element_type=jnp.float32,
    )
    grad_probs = jnp.einsum(
        "qhd,khd->hqk", grad_att_heads, vals_heads, preferred_element_type=jnp.float32
    )
    grad_scores = (
        probs_again * (grad_probs - jnp.sum(probs_again * grad_probs, axis=-1, keepdims=True))
    ).astype(jnp.bfloat16)
    grad_query = (
        jnp.einsum("hqk,khd->qhd", grad_scores, keys_heads, preferred_element_type=jnp.float32)
        * scale
    )
    grad_keys = (
        jnp.einsum("hqk,qhd->khd", grad_scores, query_heads, preferred_element_type=jnp.float32)
        * scale
    )
    grad_kv = jnp.stack([grad_keys, grad_vals]).reshape(2, document_spans, token_rows, local_width)
    carried = grad_kv[:, 0]
    carried = from_behind(carried, "wide", -1)
    carried = carried + grad_kv[:, 1]
    grad_mixed = jnp.stack(
        [grad_query.reshape(token_rows, local_width), carried[0], carried[1]], axis=1
    ).astype(jnp.bfloat16)
    grad_w_qkv = jnp.einsum(
        "td,tch->dch", normed_one, grad_mixed, preferred_element_type=jnp.float32
    )
    mixed_sums = jnp.sum(grad_mixed.astype(jnp.float32), axis=0)
    grad_b_qv = jnp.stack([mixed_sums[0], mixed_sums[2]])
    grad_norm_one = jnp.einsum("tch,dch->td", grad_mixed, w_qkv, preferred_element_type=jnp.float32)
    grad_resid_one, grad_ln1_gain, grad_ln1_bias = norm_back(
        grad_norm_one, raw_one, inv_one, ln1_gain
    )
    grad_input = (grad_mid + grad_resid_one).astype(jnp.bfloat16)
    (
        grad_ln1_gain,
        grad_ln1_bias,
        grad_w_qkv,
        grad_b_qv,
        grad_w_out,
        grad_b_out,
        grad_ln2_gain,
        grad_ln2_bias,
        grad_w_up,
        grad_b_up,
        grad_w_down,
        grad_b_down,
    ) = lax.psum(
        (
            grad_ln1_gain,
            grad_ln1_bias,
            grad_w_qkv,
            grad_b_qv,
            grad_w_out,
            grad_b_out,
            grad_ln2_gain,
            grad_ln2_bias,
            grad_w_up,
            grad_b_up,
            grad_w_down,
            grad_b_down,
        ),
        "wide",
    )
    return (
        output,
        grad_input,
        grad_ln1_gain,
        grad_ln1_bias,
        grad_w_qkv,
        grad_b_qv,
        grad_w_out,
        grad_b_out,
        grad_ln2_gain,
        grad_ln2_bias,
        grad_w_up,
        grad_b_up,
        grad_w_down,
        grad_b_down,
    )


def solution(mesh):
    return jax.shard_map(
        on_device,
        mesh=mesh,
        in_specs=(
            P("wide", None),
            P(),
            P(),
            P(None, None, "narrow"),
            P(None, "narrow"),
            P("narrow", None),
            P(),
            P(),
            P(),
            P(None, "narrow"),
            P("narrow"),
            P("narrow", None),
            P(),
            P(),
            P(),
            P(),
            P("wide", None),
        ),
        out_specs=(
            P("wide", None),
            P("wide", None),
            P(),
            P(),
            P(None, None, "narrow"),
            P(None, "narrow"),
            P("narrow", None),
            P(),
            P(),
            P(),
            P(None, "narrow"),
            P("narrow"),
            P("narrow", None),
            P(),
        ),
        check_vma=False,
    )
```

profile of v0, /device:TPU:0, one launch (start us, length us, event | category | flops | bytes accessed | tf_op | source)
XLA Modules:
  0.0 1541.9 jit_solution(12492880103837359195)
XLA Ops:
  18.7 6.4 collective-permute-start
  25.2 11.8 gather_fusion
  37.0 11.8 gather_fusion.2
  48.8 11.8 gather_fusion.1
  74.0 5.2 exponential_reduce_fusion
  79.9 6.6 convolution_convert_fusion.2
  86.5 4.7 convolution_convert_fusion
  91.3 80.2 %all-reduce.8.cloned.1.call-done = bf16[1024,2048]{1,0:T(8,128)(2,1)} async-done(((bf16[1024,2048]{1,0:T(8,128)(2,1)}), bf16[1024,2048]{1,0:T(8,128)(2,1)}) %all-reduce.8.cloned.1.call-update) | async-done | bytes 4194320 | tf_op jit(solution)/shard_map/psum | solution.py:108
  171.5 5.0 fusion.27
  189.6 7.3 convert_reduce_fusion.2
  198.2 6.8 fusion.60
  205.5 10.5 convolution_convert_fusion.1
  216.0 115.4 %all-reduce.12.cloned.1.call-done = f32[1024,2048]{1,0:T(8,128)} async-done(((f32[1024,2048]{1,0:T(8,128)}), f32[1024,2048]{1,0:T(8,128)}) %all-reduce.12.cloned.1.call-update) | async-done | bytes 8388624 | tf_op jit(solution)/shard_map/psum | solution.py:34
  331.4 8.5 multiply_reduce_fusion.1
  339.9 76.3 %all-reduce.10.cloned.1.call-done = bf16[1024,2048]{1,0:T(8,128)(2,1)} async-done(((bf16[1024,2048]{1,0:T(8,128)(2,1)}), bf16[1024,2048]{1,0:T(8,128)(2,1)}) %all-reduce.10.cloned.1.call-update) | async-done | bytes 4194320 | tf_op jit(solution)/shard_map/psum | solution.py:117
  416.2 13.9 fusion.55
  434.4 12.9 multiply_reduce_fusion
  447.3 10.1 convolution_bitcast_fusion.1
  457.3 12.4 multiply_convert_fusion
  496.5 7.1 fusion.37
  505.6 38.9 %collective-permute-done.1 = f32[2,1024,256]{2,1,0:T(8,128)} collective-permute-done((f32[2,1024,256]{2,1,0:T(8,128)}, f32[2,1024,256]{2,1,0:T(8,128)}, u32[]{:S(2)}, u32[]{:S(2)}) %collective-permute-start.1) | collective-permute-done | bytes 2097184 | tf_op jit(solution)/shard_map/ppermute | solution.py:13
  548.0 5.7 convolution_bitcast_fusion
  553.8 10.8 fusion.61
  564.6 7.6 fusion.53
  572.3 6.4 fusion.33
  578.8 6.9 fusion.41
  587.4 91.9 %all-reduce.14.cloned.1.call-done = f32[1024,2048]{1,0:T(8,128)} async-done(((f32[1024,2048]{1,0:T(8,128)}), f32[1024,2048]{1,0:T(8,128)}) %all-reduce.14.cloned.1.call-update) | async-done | bytes 8388624 | tf_op jit(solution)/shard_map/psum | solution.py:34
  679.3 6.5 fusion.15
  685.9 28.7 %all-reduce = (f32[2048]{0:T(1024)}, f32[2048]{0:T(1024)}, f32[2,256]{1,0:T(2,128)}, f32[2048]{0:T(1024)}, f32[2048]{0:T(1024)}, /*index=5*/f32[2048]{0:T(1024)}, f32[1024]{0:T(1024)}, f32[2048]{0:T(1024)}) all-reduce(f32[2048]{0:T(1024)S(1)} %get-tuple-element.17, ...), channel_id=1, replica_groups=mesh['wide'=4,'narrow'=8] {'wide'}, use_global_device_ids=true, to_apply=%region_16.18 | all-reduce | flops 13824 | bytes 110592 | tf_op jit(solution)/shard_map/psum | solution.py:191
  714.6 10.7 fusion.14
  725.3 792.0 %all-reduce.16.cloned.1.call-done = (f32[2048,3,256]{2,0,1:T(8,128)}, f32[256,2048]{1,0:T(8,128)}, f32[2048,1024]{1,0:T(8,128)}, f32[1024,2048]{1,0:T(8,128)}) async-done(((f32[2048,3,256]{2,0,1:T(8,128)}, f32[256,2048]{1,0:T(8,128)}, f32[2048,1024]{1,0:T(8,128)}, f32[1024,2048]{1,0:T(8,128)}), (f32[2048,3,256]{2,0,1:T(8,128)}, f32[256,2048]{1,0:T(8,128)}, f32[2048,1024]{1,0:T(8,128)}, ...) | async-done | bytes 25165840 | tf_op jit(solution)/shard_map/psum | solution.py:191
  1517.3 6.6 copy.64
  (176 shorter events, 89.7 us)
Async XLA Ops:
  7.2 164.2 %all-reduce.8.cloned.1.call-start = ((), (), s32[]{:S(2)}) async-start(), calls=%async_computation | async-start | bytes 8388608 | tf_op jit(solution)/shard_map/psum | solution.py:108
  16.3 8.8 copy-start.29
  16.3 8.8 copy-start.2
  18.7 47.7 %collective-permute-start = (bf16[2,1024,256]{1,2,0:T(8,128)(2,1)}, bf16[2,1024,256]{1,2,0:T(8,128)(2,1)}, u32[]{:S(2)}, u32[]{:S(2)}) collective-permute-start(bf16[2,1024,256]{1,2,0:T(8,128)(2,1)} %pad_maximum_fusion.2), channel_id=1, source_target_pairs={{0,8},{8,16},{16,24},{1,9},{9,17},{17,25},{2,10},{10,18},{18,26},{... | collective-permute-start | bytes 3145736 | tf_op jit(solution)/shard_map/ppermute | solution.py:13
  25.1 11.8 copy-start.3
  37.0 11.8 copy-start.1
  62.1 11.8 copy-start.13
  66.4 7.6 copy-start.11
  86.5 85.0 %copy-start.37 = (f32[2048]{0:T(1024)S(1)}, f32[2048]{0:T(1024)}, u32[]{:S(2)}) copy-start(f32[2048]{0:T(1024)} %param.25) | copy-start | bytes 24580
  91.2 240.2 %all-reduce.12.cloned.1.call-start = ((), (), s32[]{:S(2)}) async-start(), calls=%async_computation.2 | async-start | bytes 16777216 | tf_op jit(solution)/shard_map/psum | solution.py:34
  189.6 7.3 copy-start.53
  205.0 211.2 %all-reduce.10.cloned.1.call-start = ((), (), s32[]{:S(2)}) async-start(), calls=%async_computation.1 | async-start | bytes 8388608 | tf_op jit(solution)/shard_map/psum | solution.py:117
  215.9 200.3 %copy-start.46 = (f32[2048]{0:T(1024)S(1)}, f32[2048]{0:T(1024)}, u32[]{:S(2)}) copy-start(f32[2048]{0:T(1024)} %param.31) | copy-start | bytes 24580
  215.9 463.4 %all-reduce.14.cloned.1.call-start = ((), (), s32[]{:S(2)}) async-start(), calls=%async_computation.3 | async-start | bytes 16777216 | tf_op jit(solution)/shard_map/psum | solution.py:34
  416.2 13.9 copy-start.25
  457.3 15.8 %copy-start.14 = (f32[1024,1,256]{0,2,1:T(8,128)S(1)}, f32[1024,1,256]{0,2,1:T(8,128)}, u32[]{:S(2)}) copy-start(f32[1024,1,256]{0,2,1:T(8,128)} %copy-done.13) | copy-start | bytes 3145732
  495.2 49.3 %collective-permute-start.1 = (f32[2,1024,256]{2,1,0:T(8,128)}, f32[2,1024,256]{2,1,0:T(8,128)}, u32[]{:S(2)}, u32[]{:S(2)}) collective-permute-start(f32[2,1024,256]{2,1,0:T(8,128)} %fusion.29), channel_id=1, source_target_pairs={{8,0},{16,8},{24,16},{9,1},{17,9},{25,17},{10,2},{18,10},{26,18},{... | collective-permute-start | bytes 6291464 | tf_op jit(solution)/shard_map/ppermute | solution.py:13
  505.6 42.4 %copy-start.30 = (bf16[1024,1,256]{2,0,1:T(8,128)(2,1)S(1)}, bf16[1024,1,256]{2,0,1:T(8,128)(2,1)}, u32[]{:S(2)}) copy-start(bf16[1024,1,256]{2,0,1:T(8,128)(2,1)} %copy.47) | copy-start | bytes 1572868
  553.7 963.6 %all-reduce.16.cloned.1.call-start = ((), (), s32[]{:S(2)}) async-start(), calls=%async_computation.4 | async-start | bytes 50331648 | tf_op jit(solution)/shard_map/psum | solution.py:191
  553.8 10.8 copy-start.27
  553.8 10.8 copy-start.54
  564.6 7.6 copy-start.28
  572.2 6.5 copy-start.6
  572.2 6.5 copy-start.31
  572.2 6.5 copy-start.34
  572.2 6.5 copy-start.36
  572.3 6.5 copy-start.40
  572.3 6.5 copy-start.42
  572.3 6.5 copy-start.44
  1517.3 6.6 copy-start.32
  1517.3 8.9 copy-start.15
  1523.8 6.6 slice-start
  (33 other events, 134.7 us)
Sparse Core Ops, SparseCore 0:
  91.4 80.0 all-reduce.7
  205.1 126.2 all-reduce.11
  335.3 80.9 all-reduce.9
  553.8 125.4 all-reduce.13
  682.6 834.5 all-reduce.15
where the time goes:
time: 1550 us; the launch traced here: 1540 us
  waiting for transfers between devices  1190 us (77%)
  matrix products  120 us (8%)
  local copies, waits for them, and re-layouts  87.9 us (6%)
  other arithmetic  87 us (6%)
  blocking collectives  28.7 us (2%)
    psum x1, waiting for transfers between devices, on_device(): lax.psum((grad_ln1_gain, grad_ln1_bias, grad_w_qkv, grad_b_qv, grad_w_out...  792 us
    psum x2, waiting for transfers between devices, norm_back(): summed = lax.psum(partial_value, 'narrow')  207 us
    psum x1, waiting for transfers between devices, on_device(): lax.psum(jnp.dot(attended, w_out, preferred_element_type=jnp.float32).ast...  80.2 us
    psum x1, waiting for transfers between devices, on_device(): lax.psum(jnp.dot(active, w_down, preferred_element_type=jnp.float32).asty...  76.3 us
    ppermute x2, waiting for transfers between devices, from_behind(): lax.ppermute(value, axis, [(source, source + steps) for source in range(i...  38.9 us
    unnamed x120, local copies, waits for them, and re-layouts  31.5 us
  transfers between devices with their start and end apart: 7, of which 6 were waited for; matrix products, arithmetic and copies ran while one was open for 8% of the time, Pallas kernels for 0%

commit v1 on v0

--- a/solution.py
+++ b/solution.py
@@ -5,6 +5,15 @@
 
 HEAD_DIM = 128
 ROW_TOKENS = 2048
+
+
+def add_in_pairs(value, name):
+    size = lax.axis_size(name)
+    acc, stride = (value, 1)
+    while stride < size:
+        acc = acc + lax.ppermute(acc, name, [(i, i ^ stride) for i in range(size)])
+        stride = 2 * stride
+    return acc
 
 
 def from_behind(value, axis, steps):
@@ -31,7 +40,7 @@
 
 
 def norm_back(partial_value, normed_raw, inverse, gain):
-    summed = lax.psum(partial_value, "narrow")
+    summed = add_in_pairs(partial_value, "narrow")
     return norm_local(summed, normed_raw, inverse, gain)
 
 

time: 1550 us -> 1680 us (1.084)
  waiting for transfers between devices: 1190 us -> 1290 us
  other arithmetic: 87 us -> 144 us
    ppermute x0 -> x6, waiting for transfers between devices: none -> 773 us  [add_in_pairs(): acc = acc + lax.ppermute(acc, name, [(i, i ^ stride) for i in range(size)])]
    psum x1, waiting for transfers between devices: 792 us -> 401 us  [on_device(): lax.psum((grad_ln1_gain, grad_ln1_bias, grad_w_qkv, grad_b_qv, grad_w_out...]
    psum x2 -> x0, waiting for transfers between devices: 207 us -> none  [norm_back(): summed = lax.psum(partial_value, 'narrow')]
    psum x1, waiting for transfers between devices: 76.3 us -> 0.02 us  [on_device(): lax.psum(jnp.dot(active, w_down, preferred_element_type=jnp.float32).asty...]
    add x0 -> x4, other arithmetic: none -> 48.6 us  [add_in_pairs(): acc = acc + lax.ppermute(acc, name, [(i, i ^ stride) for i in range(size)])]
  transfers between devices with their start and end apart: 7 -> 11, of which waited for: 6 -> 8; matrix products, arithmetic and copies ran while one was open for 8% -> 9% of each run, Pallas kernels for 0% -> 0%
where the time goes in v1:
time: 1680 us
  waiting for transfers between devices  1290 us (77%)
  other arithmetic  144 us (9%)
  matrix products  111 us (7%)
  local copies, waits for them, and re-layouts  89.1 us (5%)
  blocking collectives  20.6 us (1%)
    ppermute x6, waiting for transfers between devices, add_in_pairs(): acc = acc + lax.ppermute(acc, name, [(i, i ^ stride) for i in range(size)])  773 us
    psum x1, waiting for transfers between devices, on_device(): lax.psum((grad_ln1_gain, grad_ln1_bias, grad_w_qkv, grad_b_qv, grad_w_out...  401 us
    psum x1, waiting for transfers between devices, on_device(): lax.psum(jnp.dot(attended, w_out, preferred_element_type=jnp.float32).ast...  80 us
    add x4, other arithmetic, add_in_pairs(): acc = acc + lax.ppermute(acc, name, [(i, i ^ stride) for i in range(size)])  48.6 us
  transfers between devices with their start and end apart: 11, of which 8 were waited for; matrix products, arithmetic and copies ran while one was open for 9% of the time, Pallas kernels for 0%

profile of v1, /device:TPU:0, one launch (start us, length us, event | category | flops | bytes accessed | tf_op | source)
XLA Modules:
  0.0 1676.9 jit_solution(13515087016918853114)
XLA Ops:
  18.7 6.1 collective-permute-start
  24.8 11.8 gather_fusion
  36.6 11.8 gather_fusion.2
  48.5 11.8 gather_fusion.1
  79.5 6.6 convolution_convert_fusion.2
  91.1 80.0 %all-reduce.6.cloned.1.call-done = bf16[1024,2048]{1,0:T(8,128)(2,1)} async-done(((bf16[1024,2048]{1,0:T(8,128)(2,1)}), bf16[1024,2048]{1,0:T(8,128)(2,1)}) %all-reduce.6.cloned.1.call-update) | async-done | bytes 4194320 | tf_op jit(solution)/shard_map/psum | solution.py:117
  189.0 7.9 convert_reduce_fusion.2
  204.9 13.3 collective-permute-done.1
  218.2 11.9 add.222
  231.5 181.3 %collective-permute-done.2 = f32[1024,2048]{1,0:T(8,128)} collective-permute-done((f32[1024,2048]{1,0:T(8,128)}, f32[1024,2048]{1,0:T(8,128)}, u32[]{:S(2)}, u32[]{:S(2)}) %collective-permute-start.2) | collective-permute-done | bytes 8388640 | tf_op jit(solution)/shard_map/ppermute | solution.py:14
  412.9 11.9 add.223
  426.1 10.5 convolution_convert_fusion.1
  436.6 215.0 %collective-permute-done.3 = f32[1024,2048]{1,0:T(8,128)} collective-permute-done((f32[1024,2048]{1,0:T(8,128)}, f32[1024,2048]{1,0:T(8,128)}, u32[]{:S(2)}, u32[]{:S(2)}) %collective-permute-start.3) | collective-permute-done | bytes 8388640 | tf_op jit(solution)/shard_map/ppermute | solution.py:14
  651.6 13.3 multiply_reduce_fusion.1
  665.0 13.9 fusion.55
  683.1 12.9 multiply_reduce_fusion
  696.0 10.2 convolution_bitcast_fusion.1
  706.2 12.2 multiply_convert_fusion
  745.5 9.5 fusion.61
  760.7 31.6 %collective-permute-done.4 = f32[2,1024,256]{2,1,0:T(8,128)} collective-permute-done((f32[2,1024,256]{2,1,0:T(8,128)}, f32[2,1024,256]{2,1,0:T(8,128)}, u32[]{:S(2)}, u32[]{:S(2)}) %collective-permute-start.4) | collective-permute-done | bytes 2097184 | tf_op jit(solution)/shard_map/ppermute | solution.py:22
  795.1 6.0 convolution_bitcast_fusion
  801.1 7.5 fusion.53
  811.3 7.1 fusion.41
  818.5 12.9 add.227
  832.5 182.2 %collective-permute-done.6 = f32[1024,2048]{1,0:T(8,128)} collective-permute-done((f32[1024,2048]{1,0:T(8,128)}, f32[1024,2048]{1,0:T(8,128)}, u32[]{:S(2)}, u32[]{:S(2)}) %collective-permute-start.6) | collective-permute-done | bytes 8388640 | tf_op jit(solution)/shard_map/ppermute | solution.py:14
  1014.7 12.0 add.228
  1028.1 180.8 %collective-permute-done.7 = f32[1024,2048]{1,0:T(8,128)S(1)} collective-permute-done((f32[1024,2048]{1,0:T(8,128)}, f32[1024,2048]{1,0:T(8,128)S(1)}, u32[]{:S(2)}, u32[]{:S(2)}) %collective-permute-start.7) | collective-permute-done | bytes 8388640 | tf_op jit(solution)/shard_map/ppermute | solution.py:14
  1208.9 9.9 fusion.15
  1218.8 20.6 %all-reduce = (f32[2048]{0:T(1024)}, f32[2048]{0:T(1024)}, f32[2,256]{1,0:T(2,128)}, f32[2048]{0:T(1024)}, f32[2048]{0:T(1024)}, /*index=5*/f32[2048]{0:T(1024)}, f32[1024]{0:T(1024)}, f32[2048]{0:T(1024)}) all-reduce(f32[2048]{0:T(1024)S(1)} %get-tuple-element.17, ...), channel_id=1, replica_groups=mesh['wide'=4,'narrow'=8] {'wide'}, use_global_device_ids=true, to_apply=%region_14.16 | all-reduce | flops 13824 | bytes 110592 | tf_op jit(solution)/shard_map/psum | solution.py:200
  1239.5 12.1 fusion.14
  1251.6 400.7 %all-reduce.10.cloned.1.call-done = (f32[2048,3,256]{2,0,1:T(8,128)}, f32[256,2048]{1,0:T(8,128)}, f32[2048,1024]{1,0:T(8,128)}, f32[1024,2048]{1,0:T(8,128)}) async-done(((f32[2048,3,256]{2,0,1:T(8,128)}, f32[256,2048]{1,0:T(8,128)}, f32[2048,1024]{1,0:T(8,128)}, f32[1024,2048]{1,0:T(8,128)}), (f32[2048,3,256]{2,0,1:T(8,128)}, f32[256,2048]{1,0:T(8,128)}, f32[2048,1024]{1,0:T(8,128)}, ...) | async-done | bytes 25165840 | tf_op jit(solution)/shard_map/psum | solution.py:200
  1652.3 6.6 copy.62
  (202 shorter events, 120.3 us)
Async XLA Ops:
  7.2 163.9 %all-reduce.6.cloned.1.call-start = ((), (), s32[]{:S(2)}) async-start(), calls=%async_computation | async-start | bytes 8388608 | tf_op jit(solution)/shard_map/psum | solution.py:117
  16.3 8.5 copy-start.2
  18.7 47.4 %collective-permute-start = (bf16[2,1024,256]{1,2,0:T(8,128)(2,1)}, bf16[2,1024,256]{1,2,0:T(8,128)(2,1)}, u32[]{:S(2)}, u32[]{:S(2)}) collective-permute-start(bf16[2,1024,256]{1,2,0:T(8,128)(2,1)} %pad_maximum_fusion.2), channel_id=1, source_target_pairs={{0,8},{8,16},{16,24},{1,9},{9,17},{17,25},{2,10},{10,18},{18,26},{... | collective-permute-start | bytes 3145736 | tf_op jit(solution)/shard_map/ppermute | solution.py:22
  24.8 11.8 copy-start.3
  36.6 11.8 copy-start.1
  61.7 11.8 copy-start.13
  86.1 85.0 %copy-start.38 = (f32[2048]{0:T(1024)S(1)}, f32[2048]{0:T(1024)}, u32[]{:S(2)}) copy-start(f32[2048]{0:T(1024)} %param.25) | copy-start | bytes 24580
  90.8 574.1 %all-reduce.8.cloned.1.call-start = ((), (), s32[]{:S(2)}) async-start(), calls=%async_computation.1 | async-start | bytes 8388608 | tf_op jit(solution)/shard_map/psum | solution.py:126
  204.9 13.3 collective-permute-start.1
  230.1 182.8 %collective-permute-start.2 = (f32[1024,2048]{1,0:T(8,128)}, f32[1024,2048]{1,0:T(8,128)}, u32[]{:S(2)}, u32[]{:S(2)}) collective-permute-start(f32[1024,2048]{1,0:T(8,128)} %add.222), channel_id=1, source_target_pairs={{0,2},{1,3},{2,0},{3,1},{4,6},{5,7},{6,4},{7,5},{8,10},{9,11},{10,... | collective-permute-start | bytes 25165832 | tf_op jit(solution)/shard_map/ppermute | solution.py:14
  424.7 226.9 %collective-permute-start.3 = (f32[1024,2048]{1,0:T(8,128)}, f32[1024,2048]{1,0:T(8,128)}, u32[]{:S(2)}, u32[]{:S(2)}) collective-permute-start(f32[1024,2048]{1,0:T(8,128)} %add.223), channel_id=1, source_target_pairs={{0,4},{1,5},{2,6},{3,7},{4,0},{5,1},{6,2},{7,3},{8,12},{9,13},{10,... | collective-permute-start | bytes 25165832 | tf_op jit(solution)/shard_map/ppermute | solution.py:14
  436.6 228.4 %copy-start.47 = (f32[2048]{0:T(1024)S(1)}, f32[2048]{0:T(1024)}, u32[]{:S(2)}) copy-start(f32[2048]{0:T(1024)} %param.31) | copy-start | bytes 24580
  436.6 1215.7 %all-reduce.10.cloned.1.call-start = ((), (), s32[]{:S(2)}) async-start(), calls=%async_computation.2 | async-start | bytes 50331648 | tf_op jit(solution)/shard_map/psum | solution.py:200
  665.0 13.9 copy-start.26
  706.2 15.6 copy-start.14
  740.8 14.2 slice-start.2
  744.0 11.0 slice-start.3
  744.0 11.0 copy-start.23
  744.0 48.4 %collective-permute-start.4 = (f32[2,1024,256]{2,1,0:T(8,128)}, f32[2,1024,256]{2,1,0:T(8,128)}, u32[]{:S(2)}, u32[]{:S(2)}) collective-permute-start(f32[2,1024,256]{2,1,0:T(8,128)} %fusion.29), channel_id=1, source_target_pairs={{8,0},{16,8},{24,16},{9,1},{17,9},{25,17},{10,2},{18,10},{26,18},{... | collective-permute-start | bytes 6291464 | tf_op jit(solution)/shard_map/ppermute | solution.py:22
  760.7 34.3 %copy-start.31 = (bf16[1024,1,256]{2,0,1:T(8,128)(2,1)S(1)}, bf16[1024,1,256]{2,0,1:T(8,128)(2,1)}, u32[]{:S(2)}) copy-start(bf16[1024,1,256]{2,0,1:T(8,128)(2,1)} %copy.47) | copy-start | bytes 1572868
  792.4 16.2 slice-start
  795.0 16.3 copy-start.34
  795.0 16.3 copy-start.36
  795.1 13.6 slice-start.1
  801.0 17.5 %collective-permute-start.5 = (f32[1024,2048]{1,0:T(8,128)}, f32[1024,2048]{1,0:T(8,128)}, u32[]{:S(2)}, u32[]{:S(2)}) collective-permute-start(f32[1024,2048]{1,0:T(8,128)} %convolution_bitcast_fusion), channel_id=1, source_target_pairs={{0,1},{1,0},{2,3},{3,2},{4,5},{5,4},{6,7},{7,6},{8,9},{9,8},{10,11... | collective-permute-start | bytes 25165832 | tf_op jit(solution)/shard_map/ppermute | solution.py:14
  831.4 196.4 %copy-start.32 = (bf16[1024,1,256]{2,0,1:T(8,128)(2,1)S(1)}, bf16[1024,1,256]{2,0,1:T(8,128)(2,1)}, u32[]{:S(2)}) copy-start(bf16[1024,1,256]{2,0,1:T(8,128)(2,1)} %copy.47) | copy-start | bytes 1572868
  831.4 196.4 %copy-start.35 = (bf16[1024,1,256]{2,0,1:T(8,128)(2,1)S(1)}, bf16[1024,1,256]{2,0,1:T(8,128)(2,1)}, u32[]{:S(2)}) copy-start(bf16[1024,1,256]{2,0,1:T(8,128)(2,1)} %copy-done.34) | copy-start | bytes 1572868
  831.4 196.4 %copy-start.37 = (bf16[1024,1,256]{2,0,1:T(8,128)(2,1)S(1)}, bf16[1024,1,256]{2,0,1:T(8,128)(2,1)}, u32[]{:S(2)}) copy-start(bf16[1024,1,256]{2,0,1:T(8,128)(2,1)} %copy-done.36) | copy-start | bytes 1572868
  831.4 183.3 %collective-permute-start.6 = (f32[1024,2048]{1,0:T(8,128)}, f32[1024,2048]{1,0:T(8,128)}, u32[]{:S(2)}, u32[]{:S(2)}) collective-permute-start(f32[1024,2048]{1,0:T(8,128)} %add.227), channel_id=1, source_target_pairs={{0,2},{1,3},{2,0},{3,1},{4,6},{5,7},{6,4},{7,5},{8,10},{9,11},{10,... | collective-permute-start | bytes 25165832 | tf_op jit(solution)/shard_map/ppermute | solution.py:14
  1026.6 182.3 %collective-permute-start.7 = (f32[1024,2048]{1,0:T(8,128)}, f32[1024,2048]{1,0:T(8,128)S(1)}, u32[]{:S(2)}, u32[]{:S(2)}) collective-permute-start(f32[1024,2048]{1,0:T(8,128)} %add.228), channel_id=1, source_target_pairs={{0,4},{1,5},{2,6},{3,7},{4,0},{5,1},{6,2},{7,3},{8,12},{9,13},{10,... | collective-permute-start | bytes 25165832 | tf_op jit(solution)/shard_map/ppermute | solution.py:14
  1028.1 190.8 %copy-start.48 = (f32[1024]{0:T(1024)S(1)}, f32[1024]{0:T(1024)}, u32[]{:S(2)}) copy-start(f32[1024]{0:T(1024)} %get-tuple-element.35) | copy-start | bytes 12292
  1652.3 8.9 copy-start.16
  (44 other events, 203.1 us)
Sparse Core Ops, SparseCore 0:
  91.0 80.0 all-reduce.5
  436.7 126.2 all-reduce.7
  818.6 833.6 all-reduce.9
